TPU v7x, 256 devices: a whole 4x4x8 slice. The times are simulated.
256 devices in a mesh: branch: 2 (over core), pair: 128 (over y, x, z).
Axes of the slice: x: 4, y: 4, z: 8, core: 2. Of those that a mesh axis runs over, the one named last changes fastest.
Arguments:
- encoder_rows: bfloat16 [256, 196, 1024], P('pair'), may hold values from -6 to 6
- pair_list: int32 [512, 2], P('pair'), may hold values from 0 to 255, as said below
- embed_weight: bfloat16 [1024, 768], P('pair'), may hold values from -0.1875 to 0.1875
- self_qkv: bfloat16 [2, 768, 2304], P('branch'), may hold values from -0.21875 to 0.21875
- self_out: bfloat16 [2, 768, 768], P('branch'), may hold values from -0.21875 to 0.21875
- cross_q: bfloat16 [2, 768, 768], P('branch'), may hold values from -0.21875 to 0.21875
- cross_kv: bfloat16 [2, 768, 1536], P('branch'), may hold values from -0.21875 to 0.21875
- cross_out: bfloat16 [2, 768, 768], P('branch'), may hold values from -0.21875 to 0.21875
Outputs:
- view_sums: float32 [2, 256, 196, 768], P('branch', 'pair')
Inputs may be any that keep to these rules, and one draw needn't show every extreme that they name: `pair_list`: pair p's first image (column 0) is one of the images p // 4 * 2 to p // 4 * 2 + 1, and every image is the first image of some pair. The second image (column 1) differs from the first and is one of the images (p // 4 - 1) * 2 to (p // 4 + 2) * 2 - 1, counted modulo 256; where p % 4 is 0 it is one of the images (p // 4 + 1) * 2 to (p // 4 + 2) * 2 - 1, and where p % 4 is 1 one of the images (p // 4 - 1) * 2 to p // 4 * 2 - 1, both modulo 256.
All inputs are finite; a program needn't handle non-finite values.
Results may differ from a plain program's by a relative error of at most 0.0034.
Values may be sent and summed in bfloat16 or wider, within the bound.
A program may use at most 64 MiB of HBM per device.

v0:
```python
import math
import jax
import jax.numpy as jnp
from jax import lax
from jax.sharding import PartitionSpec as P

HEADS = 12


def padded(x, sides, width):
    for axis, dim in sides:
        peers, length = (lax.axis_size(axis), x.shape[dim])
        up = [(i, (i + 1) % peers) for i in range(peers)]
        down = [(j, i) for i, j in up]
        last = lax.slice_in_dim(x, length - width, length, axis=dim)
        initial = lax.slice_in_dim(x, 0, width, axis=dim)
        before = lax.ppermute(last, axis, up)
        after = lax.ppermute(initial, axis, down)
        x = jnp.concatenate([before, x, after], axis=dim)
    return x


def swapped(value, axis, bit):
    mask = 2**bit
    pairs = [(source, source ^ mask) for source in range(lax.axis_size(axis))]
    return lax.ppermute(value, axis, pairs)


def layer_norm(values):
    values = values.astype(jnp.float32)
    average = jnp.mean(values, axis=-1, keepdims=True)
    centered = values - average
    spread = jnp.mean(centered * centered, axis=-1, keepdims=True)
    return (centered * lax.rsqrt(spread + 1e-06)).astype(jnp.bfloat16)


def project(values, matrix):
    leading = values.shape[:-1]
    flattened = values.reshape(-1, values.shape[-1])
    result = jnp.dot(flattened, matrix, preferred_element_type=jnp.float32)
    return result.reshape(leading + (matrix.shape[-1],))


def attend(queries, keys_in, values_in):
    pair_count, length, model_width = queries.shape
    head_dim = model_width // HEADS
    query_heads = queries.reshape(pair_count, length, HEADS, head_dim)
    key_heads = keys_in.reshape(pair_count, length, HEADS, head_dim)
    value_heads = values_in.reshape(pair_count, length, HEADS, head_dim)
    scores = jnp.einsum(
        "bqhd,bkhd->bhqk", query_heads, key_heads, preferred_element_type=jnp.float32
    ) * (1.0 / math.sqrt(head_dim))
    raised = jnp.exp(scores)
    attn_probs = (raised / jnp.sum(raised, axis=-1, keepdims=True)).astype(jnp.bfloat16)
    mixed_rows = jnp.einsum(
        "bhqk,bkhd->bqhd", attn_probs, value_heads, preferred_element_type=jnp.float32
    )
    return mixed_rows.reshape(pair_count, length, model_width).astype(jnp.bfloat16)


def attention_part(own_rows, partner_rows, w_qkv, w_self, w_query, w_pair, w_cross):
    model_width = own_rows.shape[-1]
    triple = project(layer_norm(own_rows), w_qkv).astype(jnp.bfloat16)
    attended = attend(
        triple[..., :model_width],
        triple[..., model_width : 2 * model_width],
        triple[..., 2 * model_width :],
    )
    stream = own_rows.astype(jnp.float32) + project(attended, w_self)
    query_rows = project(layer_norm(stream), w_query).astype(jnp.bfloat16)
    pair_kv = project(layer_norm(partner_rows), w_pair).astype(jnp.bfloat16)
    crossed = attend(query_rows, pair_kv[..., :model_width], pair_kv[..., model_width:])
    return stream + project(crossed, w_cross)


def select_rows(onehot, window):
    return jnp.dot(onehot.astype(jnp.bfloat16), window, preferred_element_type=jnp.float32).astype(
        jnp.bfloat16
    )


def embed_picked(onehot, window, full_embed, pair_count, tokens_per, enc_width, model_width):
    picked = select_rows(onehot, window).reshape(pair_count * tokens_per, enc_width)
    embedded_rows = jnp.dot(picked, full_embed, preferred_element_type=jnp.float32).astype(
        jnp.bfloat16
    )
    return embedded_rows.reshape(pair_count, tokens_per, model_width)


def body(encoder_rows, pair_list, embed_weight, self_qkv, self_out, cross_q, cross_kv, cross_out):
    img_local = encoder_rows.shape[0]
    tokens_per = encoder_rows.shape[1]
    enc_width = encoder_rows.shape[2]
    pair_count = pair_list.shape[0]
    views_local = self_qkv.shape[0]
    devices = lax.axis_size("pair")
    device_id = lax.axis_index("pair")
    branch_id = lax.axis_index("branch")
    image_total = img_local * devices
    window_start = (device_id - 1) * img_local
    slot_index = jnp.arange(3 * img_local, dtype=jnp.int32)
    other_onehots = []
    local_view = 0
    view_id = branch_id * views_local + local_view
    own_ids = jnp.where(view_id == 0, pair_list[:, 0], pair_list[:, 1])
    other_ids = jnp.where(view_id == 0, pair_list[:, 1], pair_list[:, 0])
    own_place = jnp.mod(own_ids - window_start, image_total)
    other_place = jnp.mod(other_ids - window_start, image_total)
    own_places = [own_place]
    own_onehots = own_place[:, None] == slot_index[None, :]
    other_onehots.append(other_place[:, None] == slot_index[None, :])
    full_embed = lax.all_gather(embed_weight, "pair", axis=0, tiled=True)
    model_width = full_embed.shape[1]
    raw_local = encoder_rows.reshape(img_local, tokens_per * enc_width)
    window = padded(raw_local, (("pair", 0),), img_local)
    own_list = [
        embed_picked(
            own_onehots, window, full_embed, pair_count, tokens_per, enc_width, model_width
        )
    ]
    partner_list = [swapped(own_list[0], "branch", 0)]
    local_view = 0
    decoded = attention_part(
        own_list[local_view],
        partner_list[local_view],
        self_qkv[local_view],
        self_out[local_view],
        cross_q[local_view],
        cross_kv[local_view],
        cross_out[local_view],
    )
    place_onehot = (slot_index[:, None] == own_places[local_view][None, :]).astype(jnp.float32)
    contribution_list = [
        jnp.dot(
            place_onehot,
            decoded.reshape(pair_count, tokens_per * model_width),
            precision=lax.Precision.HIGHEST,
        )
    ]
    contributions = jnp.stack(contribution_list, axis=0)
    rim_rows = jnp.concatenate(
        [contributions[:, :img_local], contributions[:, 2 * img_local :]], axis=1
    )
    extended = padded(rim_rows, (("pair", 1),), img_local)
    image_sums = (
        contributions[:, img_local : 2 * img_local]
        + extended[:, :img_local]
        + extended[:, 3 * img_local :]
    )
    return image_sums.reshape(views_local, img_local, tokens_per, model_width)


def solution(mesh):
    placed = (
        P("pair", None, None),
        P("pair", None),
        P("pair", None),
        P("branch", None, None),
        P("branch", None, None),
        P("branch", None, None),
        P("branch", None, None),
        P("branch", None, None),
    )
    return jax.shard_map(
        body, mesh=mesh, in_specs=placed, out_specs=P("branch", "pair", None, None), check_vma=False
    )
```

profile of v0, /device:TPU:1, one launch (start us, length us, event | category | flops | bytes accessed | tf_op | source)
XLA Modules:
  0.0 225.7 jit_solution(11989858726416793992)
XLA Ops:
  7.3 2.5 %collective-permute-start = (bf16[2,200704]{1,0:T(2,128)(2,1)}, bf16[2,200704]{1,0:T(2,128)(2,1)}, u32[]{:S(2)}, u32[]{:S(2)}) collective-permute-start(bf16[2,200704]{1,0:T(2,128)(2,1)} %bitcast.65), channel_id=1, source_target_pairs={{0,1},{1,2},{2,3},{3,4},{4,5},{5,6},{6,7},{7,8},{8,9},{9,10},{10,1... | collective-permute-start | bytes 2408456 | tf_op jit(solution)/shard_map/ppermute | solution.py:17
  9.8 8.7 %collective-permute-start.1 = (bf16[2,200704]{1,0:T(2,128)(2,1)}, bf16[2,200704]{1,0:T(2,128)(2,1)}, u32[]{:S(2)}, u32[]{:S(2)}) collective-permute-start(bf16[2,200704]{1,0:T(2,128)(2,1)} %bitcast.66), channel_id=1, source_target_pairs={{1,0},{2,1},{3,2},{4,3},{5,4},{6,5},{7,6},{8,7},{9,8},{10,9},{11,1... | collective-permute-start | bytes 2408456 | tf_op jit(solution)/shard_map/ppermute | solution.py:18
  19.2 17.0 %collective-permute-done = bf16[2,200704]{1,0:T(2,128)(2,1)} collective-permute-done((bf16[2,200704]{1,0:T(2,128)(2,1)}, bf16[2,200704]{1,0:T(2,128)(2,1)}, u32[]{:S(2)}, u32[]{:S(2)}) %collective-permute-start) | collective-permute-done | bytes 802848 | tf_op jit(solution)/shard_map/ppermute | solution.py:17
  36.3 5.6 %convolution_convert_fusion = bf16[4,200704]{1,0:T(4,128)(2,1)} fusion(bf16[2,200704]{1,0:T(2,128)(2,1)} %collective-permute-done.1, bf16[2,200704]{1,0:T(2,128)(2,1)} %bitcast.67, bf16[2,200704]{1,0:T(2,128)(2,1)} %collective-permute-done, s32[4]{0:T(128)S(1)} %fusion.31), kind=kOutput, calls=%fused_computation | convolution fusion | flops 17661976 | bytes 4014096 | tf_op jit(solution)/shard_map/dot_general | solution.py:77
  41.9 3.6 %reshape.134 = bf16[784,1024]{1,0:T(8,128)(2,1)} reshape(bf16[4,200704]{1,0:T(4,128)(2,1)} %convolution_convert_fusion) | data formatting | bytes 3211264 | tf_op jit(solution)/shard_map/reshape | solution.py:83
  45.5 68.6 %all-gather.2.cloned.1.call-done = bf16[1024,768]{1,0:T(8,128)(2,1)} async-done(((bf16[8,768]{1,0:T(8,128)(2,1)}), bf16[1024,768]{1,0:T(8,128)(2,1)}) %all-gather.2.cloned.1.call-update) | async-done | bytes 1572880 | tf_op jit(solution)/shard_map/all_gather | solution.py:112
  114.0 4.3 %convert_reduce_fusion.1 = (f32[784]{0:T(1024)S(1)}, bf16[784,768]{1,0:T(8,128)(2,1)}) fusion(bf16[784,1024]{1,0:T(8,128)(2,1)} %reshape.134, bf16[1024,768]{1,0:T(8,128)(2,1)} %all-gather.2.cloned.1.call-done), kind=kOutput, calls=%fused_computation.21 | convolution fusion | flops 1234930944 | bytes 4385856 | tf_op jit(solution)/shard_map/dot_general | solution.py:84
  118.4 2.2 reshape.135
  120.6 1.8 fusion.16
  122.4 2.7 %fusion.17 = bf16[784,768]{1,0:T(8,128)(2,1)} fusion(bf16[784,768]{1,0:T(8,128)(2,1)} %get-tuple-element.15, f32[784]{0:T(1024)S(1)} %add_rsqrt_fusion.2, f32[784]{0:T(1024)S(1)} %broadcast_multiply_fusion.2), kind=kLoop, calls=%fused_computation.33 | loop fusion | flops 2408448 | bytes 2414720 | tf_op jit(solution)/shard_map/convert_element_type | solution.py:34
  125.1 2.2 dot_general.40
  127.3 4.8 %convolution_convert_fusion.1 = bf16[4,196,2304]{2,1,0:T(8,128)(2,1)S(1)} fusion(bf16[4,196,768]{2,1,0:T(8,128)(2,1)} %dot_general.40, bf16[1,768,2304]{2,1,0:T(8,128)(2,1)S(1)} %copy-done), kind=kOutput, calls=%fused_computation.8 | convolution fusion | flops 2776338432 | bytes 8355840 | tf_op jit(solution)/shard_map/dot_general | solution.py:40
  132.1 1.9 fusion.39
  134.0 1.6 copy.78
  135.7 2.5 %copy.79 = bf16[4,196,768]{1,2,0:T(8,128)(2,1)} copy(bf16[4,196,768]{2,1,0:T(8,128)(2,1)} %get-tuple-element.9) | data formatting | bytes 2408448 | tf_op jit(solution)/shard_map/slice | solution.py:66
  138.2 2.5 %copy.77 = bf16[4,196,768]{1,2,0:T(8,128)(2,1)} copy(bf16[4,196,768]{2,1,0:T(8,128)(2,1)} %get-tuple-element.11) | data formatting | bytes 2408448 | tf_op jit(solution)/shard_map/slice | solution.py:67
  140.7 2.9 %copy.82 = bf16[4,196,768]{2,0,1:T(4,128)(2,1)} copy(bf16[4,196,768]{2,1,0:T(8,128)(2,1)} %reshape.135) | data formatting | bytes 2408448 | tf_op jit(solution)/shard_map/reshape | solution.py:87
  143.6 4.8 %collective-permute-start.2 = (bf16[4,196,768]{2,0,1:T(4,128)(2,1)}, bf16[4,196,768]{2,0,1:T(4,128)(2,1)S(1)}, u32[]{:S(2)}, u32[]{:S(2)}) collective-permute-start(bf16[4,196,768]{2,0,1:T(4,128)(2,1)} %copy.82), channel_id=1, source_target_pairs={{0,128},{128,0},{1,129},{129,1},{2,130},{130,2},{3,131},{131,3},{4... | collective-permute-start | bytes 3612680 | tf_op jit(solution)/shard_map/ppermute | solution.py:26
  148.4 2.1 fusion
  150.5 2.2 fusion.20
  156.2 2.3 %convolution_convert_fusion.3 = bf16[4,196,768]{2,1,0:T(8,128)(2,1)} fusion(f32[4,196,768]{2,1,0:T(8,128)S(1)} %get-tuple-element.19, f32[4,196]{1,0:T(4,128)S(1)} %add_rsqrt_fusion.1, f32[4,196]{1,0:T(4,128)S(1)} %broadcast_multiply_fusion.1, bf16[1,768,768]{2,1,0:T(8,128)(2,1)S(1)} %copy-done.11), kind=kOutput, calls=%fused_computation.37 | convolution fusion | flops 927252480 | bytes 4798592 | tf_op jit(solution)/shard_map/dot_general | solution.py:40
  158.5 1.6 copy.89
  162.8 2.1 convolution_convert_fusion.2
  164.9 1.6 fusion.40
  166.5 2.5 %copy.90 = bf16[4,196,768]{1,2,0:T(8,128)(2,1)} copy(bf16[4,196,768]{2,1,0:T(8,128)(2,1)} %get-tuple-element.12) | data formatting | bytes 2408448 | tf_op jit(solution)/shard_map/slice | solution.py:72
  169.0 2.5 %copy.88 = bf16[4,196,768]{1,2,0:T(8,128)(2,1)} copy(bf16[4,196,768]{2,1,0:T(8,128)(2,1)} %get-tuple-element.13) | data formatting | bytes 2408448 | tf_op jit(solution)/shard_map/slice | solution.py:72
  171.6 3.7 %fusion.1 = (f32[4,12,196]{2,1,0:T(8,128)S(1)}, f32[4,12,196,196]{2,3,1,0:T(8,128)S(1)}) fusion(bf16[4,196,12,64]{1,3,2,0:T(8,128)(2,1)S(1)} %bitcast.58, bf16[4,196,12,64]{1,3,2,0:T(8,128)(2,1)} %bitcast.61), kind=kOutput, calls=%fused_computation.7 | convolution fusion | flops 239706432 | bytes 9821952 | tf_op jit(solution)/shard_map/bqhd,bkhd->bhqk/dot_general | solution.py:50
  175.3 2.4 %fusion.19 = bf16[4,12,64,196]{3,2,1,0:T(8,128)(2,1)S(1)} fusion(bf16[4,196,12,64]{1,3,2,0:T(8,128)(2,1)S(1)} %bitcast.63, f32[4,12,196,196]{2,3,1,0:T(8,128)S(1)} %get-tuple-element.21, f32[4,12,196]{2,1,0:T(8,128)S(1)} %get-tuple-element.20), kind=kOutput, calls=%fused_computation.35 | convolution fusion | flops 242161920 | bytes 9821952 | tf_op jit(solution)/shard_map/bhqk,bkhd->bqhd/dot_general | solution.py:55
  179.8 2.4 %convolution_bitcast_fusion = f32[1,6,150528]{2,1,0:T(8,128)S(1)} fusion(f32[4,150528]{1,0:T(4,128)S(1)} %bitcast.57, s32[4]{0:T(128)S(1)} %get-tuple-element.5), kind=kOutput, calls=%fused_computation.1 | convolution fusion | flops 43352088 | bytes 6021136 | tf_op jit(solution)/shard_map/dot_general | solution.py:134
  184.4 5.8 %collective-permute-start.4 = (f32[1,2,150528]{2,1,0:T(2,128)S(1)}, f32[1,2,150528]{2,1,0:T(2,128)S(1)}, u32[]{:S(2)}, u32[]{:S(2)}) collective-permute-start(f32[1,2,150528]{2,1,0:T(2,128)S(1)} %get-tuple-element.8), channel_id=1, source_target_pairs={{1,0},{2,1},{3,2},{4,3},{5,4},{6,5},{7,6},{8,7},{9,8},{10,9},{11,1... | collective-permute-start | bytes 3612680 | tf_op jit(solution)/shard_map/ppermute | solution.py:18
  190.2 26.6 %collective-permute-done.3 = f32[1,2,150528]{2,1,0:T(2,128)S(1)} collective-permute-done((f32[1,2,150528]{2,1,0:T(2,128)S(1)}, f32[1,2,150528]{2,1,0:T(2,128)S(1)}, u32[]{:S(2)}, u32[]{:S(2)}) %collective-permute-start.3) | collective-permute-done | bytes 1204256 | tf_op jit(solution)/shard_map/ppermute | solution.py:17
  216.8 2.0 fusion.24
  (46 shorter events, 11.9 us)
Async XLA Ops:
  6.5 120.8 %copy-start = (bf16[1,768,2304]{2,1,0:T(8,128)(2,1)S(1)}, bf16[1,768,2304]{2,1,0:T(8,128)(2,1)}, u32[]{:S(2)}) copy-start(bf16[1,768,2304]{2,1,0:T(8,128)(2,1)} %param.11) | copy-start | bytes 10616836
  6.5 107.5 %all-gather.2.cloned.1.call-start = ((), (), s32[]{:S(2)}) async-start(), calls=%async_computation | async-start | bytes 1585152 | tf_op jit(solution)/shard_map/all_gather | solution.py:112
  7.3 29.0 %collective-permute-start = (bf16[2,200704]{1,0:T(2,128)(2,1)}, bf16[2,200704]{1,0:T(2,128)(2,1)}, u32[]{:S(2)}, u32[]{:S(2)}) collective-permute-start(bf16[2,200704]{1,0:T(2,128)(2,1)} %bitcast.65), channel_id=1, source_target_pairs={{0,1},{1,2},{2,3},{3,4},{4,5},{5,6},{6,7},{7,8},{8,9},{9,10},{10,1... | collective-permute-start | bytes 2408456 | tf_op jit(solution)/shard_map/ppermute | solution.py:17
  9.8 26.5 %collective-permute-start.1 = (bf16[2,200704]{1,0:T(2,128)(2,1)}, bf16[2,200704]{1,0:T(2,128)(2,1)}, u32[]{:S(2)}, u32[]{:S(2)}) collective-permute-start(bf16[2,200704]{1,0:T(2,128)(2,1)} %bitcast.66), channel_id=1, source_target_pairs={{1,0},{2,1},{3,2},{4,3},{5,4},{6,5},{7,6},{8,7},{9,8},{10,9},{11,1... | collective-permute-start | bytes 2408456 | tf_op jit(solution)/shard_map/ppermute | solution.py:18
  140.7 7.7 %copy-start.4 = (bf16[4,196,768]{1,2,0:T(8,128)(2,1)S(1)}, bf16[4,196,768]{1,2,0:T(8,128)(2,1)}, u32[]{:S(2)}) copy-start(bf16[4,196,768]{1,2,0:T(8,128)(2,1)} %copy.79) | copy-start | bytes 3612676
  143.6 16.5 %collective-permute-start.2 = (bf16[4,196,768]{2,0,1:T(4,128)(2,1)}, bf16[4,196,768]{2,0,1:T(4,128)(2,1)S(1)}, u32[]{:S(2)}, u32[]{:S(2)}) collective-permute-start(bf16[4,196,768]{2,0,1:T(4,128)(2,1)} %copy.82), channel_id=1, source_target_pairs={{0,128},{128,0},{1,129},{129,1},{2,130},{130,2},{3,131},{131,3},{4... | collective-permute-start | bytes 3612680 | tf_op jit(solution)/shard_map/ppermute | solution.py:26
  148.4 2.1 copy-start.6
  150.5 2.2 copy-start.5
  150.5 2.2 copy-start.10
  154.1 1.4 copy-start.2
  154.1 2.1 copy-start.11
  160.7 2.1 copy-start.9
  171.6 3.7 %copy-start.7 = (bf16[4,196,768]{1,2,0:T(8,128)(2,1)S(1)}, bf16[4,196,768]{1,2,0:T(8,128)(2,1)}, u32[]{:S(2)}) copy-start(bf16[4,196,768]{1,2,0:T(8,128)(2,1)} %copy.88) | copy-start | bytes 3612676
  175.2 2.4 %copy-start.3 = (f32[4,196,768]{2,1,0:T(8,128)S(1)}, f32[4,196,768]{2,1,0:T(8,128)}, u32[]{:S(2)}) copy-start(f32[4,196,768]{2,1,0:T(8,128)} %copy-done.2) | copy-start | bytes 7225348
  175.3 2.4 %copy-start.8 = (bf16[1,768,768]{2,1,0:T(8,128)(2,1)S(1)}, bf16[1,768,768]{2,1,0:T(8,128)(2,1)}, u32[]{:S(2)}) copy-start(bf16[1,768,768]{2,1,0:T(8,128)(2,1)} %param.15) | copy-start | bytes 3538948
  183.3 33.6 %collective-permute-start.3 = (f32[1,2,150528]{2,1,0:T(2,128)S(1)}, f32[1,2,150528]{2,1,0:T(2,128)S(1)}, u32[]{:S(2)}, u32[]{:S(2)}) collective-permute-start(f32[1,2,150528]{2,1,0:T(2,128)S(1)} %get-tuple-element.7), channel_id=1, source_target_pairs={{0,1},{1,2},{2,3},{3,4},{4,5},{5,6},{6,7},{7,8},{8,9},{9,10},{10,1... | collective-permute-start | bytes 3612680 | tf_op jit(solution)/shard_map/ppermute | solution.py:17
  184.4 34.4 %copy-start.1 = (bf16[1,768,2304]{2,1,0:T(8,128)(2,1)S(1)}, bf16[1,768,2304]{2,1,0:T(8,128)(2,1)}, u32[]{:S(2)}) copy-start(bf16[1,768,2304]{2,1,0:T(8,128)(2,1)} %param.11) | copy-start | bytes 10616836
  184.4 32.4 %collective-permute-start.4 = (f32[1,2,150528]{2,1,0:T(2,128)S(1)}, f32[1,2,150528]{2,1,0:T(2,128)S(1)}, u32[]{:S(2)}, u32[]{:S(2)}) collective-permute-start(f32[1,2,150528]{2,1,0:T(2,128)S(1)} %get-tuple-element.8), channel_id=1, source_target_pairs={{1,0},{2,1},{3,2},{4,3},{5,4},{6,5},{7,6},{8,7},{9,8},{10,9},{11,1... | collective-permute-start | bytes 3612680 | tf_op jit(solution)/shard_map/ppermute | solution.py:18
Sparse Core Ops, SparseCore 0:
  10.8 103.2 all-gather.1
where the time goes:
time: 226 us
  waiting for transfers between devices  113 us (50%)
  matrix products  34.4 us (15%)
  local copies, waits for them, and re-layouts  31.5 us (14%)
  starting transfers between devices  23 us (10%)
  between operations  13.7 us (6%)
  other arithmetic  10.3 us (5%)
    all_gather x1, waiting for transfers between devices, body(): full_embed = lax.all_gather(embed_weight, 'pair', axis=0, tiled=True)  68.6 us
    ppermute x2, waiting for transfers between devices, padded(): before = lax.ppermute(last, axis, up)  43.6 us
    ppermute x2, starting transfers between devices, padded(): after = lax.ppermute(initial, axis, down)  14.5 us
    dot_general x5, matrix products, project(): result = jnp.dot(flattened, matrix, preferred_element_type=jnp.float32)  11.8 us
    dot_general x2, matrix products, attend(): jnp.einsum('bqhd,bkhd->bhqk', query_heads, key_heads, preferred_element_t...  5.76 us
    dot_general x1, matrix products, select_rows(): jnp.dot(onehot.astype(jnp.bfloat16), window, preferred_element_type=jnp.f...  5.59 us
    reshape x2, local copies, waits for them, and re-layouts, embed_picked(): return embedded_rows.reshape(pair_count, tokens_per, model_width)  5.13 us
    ppermute x1, starting transfers between devices, swapped(): return lax.ppermute(value, axis, pairs)  4.77 us
  transfers between devices with their start and end apart: 6, of which 3 were waited for; matrix products, arithmetic and copies ran while one was open for 9% of the time, Pallas kernels for 0%

commit v1 on v0

--- a/solution.py
+++ b/solution.py
@@ -5,6 +5,13 @@
 from jax.sharding import PartitionSpec as P
 
 HEADS = 12
+
+
+def exchange_gather(value, axis, d):
+    count = lax.axis_size(axis)
+    shards = jnp.stack([value for _ in range(count)])
+    shards = lax.all_to_all(shards, axis, split_axis=0, concat_axis=0)
+    return jnp.concatenate(shards, axis=d)
 
 
 def padded(x, sides, width):
@@ -109,7 +116,7 @@
     own_places = [own_place]
     own_onehots = own_place[:, None] == slot_index[None, :]
     other_onehots.append(other_place[:, None] == slot_index[None, :])
-    full_embed = lax.all_gather(embed_weight, "pair", axis=0, tiled=True)
+    full_embed = exchange_gather(embed_weight, "pair", 0)
     model_width = full_embed.shape[1]
     raw_local = encoder_rows.reshape(img_local, tokens_per * enc_width)
     window = padded(raw_local, (("pair", 0),), img_local)

time: 226 us -> 187 us (0.83)
  waiting for transfers between devices: 113 us -> 76.2 us
  between operations: 13.7 us -> 0.29 us
  starting transfers between devices: 23 us -> 32.5 us
  local copies, waits for them, and re-layouts: 31.5 us -> 34.3 us
    all_gather x1 -> x0, waiting for transfers between devices: 68.6 us -> none  [body(): full_embed = lax.all_gather(embed_weight, 'pair', axis=0, tiled=True)]
    ppermute x2, waiting for transfers between devices: 43.6 us -> 76.2 us  [padded(): before = lax.ppermute(last, axis, up)]
    all_to_all x0 -> x1, starting transfers between devices: none -> 16.9 us  [exchange_gather(): shards = lax.all_to_all(shards, axis, split_axis=0, concat_axis=0)]
    ppermute x1, starting transfers between devices: 4.77 us -> 1.55 us  [swapped(): return lax.ppermute(value, axis, pairs)]
    ppermute x2, starting transfers between devices: 3.7 us -> 0.67 us  [padded(): before = lax.ppermute(last, axis, up)]
  transfers between devices with their start and end apart: 6 -> 6, of which waited for: 3 -> 2; matrix products, arithmetic and copies ran while one was open for 9% -> 10% of each run, Pallas kernels for 0% -> 0%
where the time goes in v1:
time: 187 us; the launch traced here: 186 us
  waiting for transfers between devices  76.2 us (41%)
  matrix products  34.6 us (19%)
  local copies, waits for them, and re-layouts  34.3 us (18%)
  starting transfers between devices  32.5 us (17%)
  other arithmetic  8.38 us (4%)
    ppermute x2, waiting for transfers between devices, padded(): before = lax.ppermute(last, axis, up)  76.2 us
    all_to_all x1, starting transfers between devices, exchange_gather(): shards = lax.all_to_all(shards, axis, split_axis=0, concat_axis=0)  16.9 us
    ppermute x2, starting transfers between devices, padded(): after = lax.ppermute(initial, axis, down)  13.3 us
    dot_general x5, matrix products, project(): result = jnp.dot(flattened, matrix, preferred_element_type=jnp.float32)  11.8 us
    dot_general x2, matrix products, attend(): jnp.einsum('bqhd,bkhd->bhqk', query_heads, key_heads, preferred_element_t...  5.75 us
    dot_general x1, matrix products, select_rows(): jnp.dot(onehot.astype(jnp.bfloat16), window, preferred_element_type=jnp.f...  5.58 us
    reshape x2, local copies, waits for them, and re-layouts, embed_picked(): return embedded_rows.reshape(pair_count, tokens_per, model_width)  5.15 us
    dot_general x2, matrix products, attend(): jnp.einsum('bhqk,bkhd->bqhd', attn_probs, value_heads, preferred_element_...  4.79 us
  transfers between devices with their start and end apart: 6, of which 2 were waited for; matrix products, arithmetic and copies ran while one was open for 10% of the time, Pallas kernels for 0%

profile of v1, /device:TPU:1, one launch (start us, length us, event | category | flops | bytes accessed | tf_op | source)
XLA Modules:
  0.0 186.3 jit_solution(11980038494513568980)
XLA Ops:
  0.0 2.1 %stack.4 = bf16[128,8,768]{2,1,0:T(8,128)(2,1)} broadcast(bf16[8,768]{1,0:T(8,128)(2,1)} %param.10), dimensions={1,2} | broadcast | bytes 1585152 | tf_op jit(solution)/shard_map/stack | solution.py:12
  2.1 16.9 %all-to-all-start = ((bf16[128,8,768]{2,1,0:T(8,128)(2,1)}), bf16[128,8,768]{2,1,0:T(8,128)(2,1)}, u32[]{:S(2)}, u32[]{:S(2)}) async-start(bf16[128,8,768]{2,1,0:T(8,128)(2,1)} %stack.4), calls=%async_computation | async-start | bytes 3145728 | tf_op jit(solution)/shard_map/all_to_all | solution.py:13
  19.6 6.5 %collective-permute-start.1 = (bf16[2,200704]{1,0:T(2,128)(2,1)}, bf16[2,200704]{1,0:T(2,128)(2,1)}, u32[]{:S(2)}, u32[]{:S(2)}) collective-permute-start(bf16[2,200704]{1,0:T(2,128)(2,1)} %bitcast.72), channel_id=1, source_target_pairs={{1,0},{2,1},{3,2},{4,3},{5,4},{6,5},{7,6},{8,7},{9,8},{10,9},{11,1... | collective-permute-start | bytes 2408456 | tf_op jit(solution)/shard_map/ppermute | solution.py:25
  26.1 49.7 %collective-permute-done = bf16[2,200704]{1,0:T(2,128)(2,1)} collective-permute-done((bf16[2,200704]{1,0:T(2,128)(2,1)}, bf16[2,200704]{1,0:T(2,128)(2,1)}, u32[]{:S(2)}, u32[]{:S(2)}) %collective-permute-start) | collective-permute-done | bytes 802848 | tf_op jit(solution)/shard_map/ppermute | solution.py:24
  75.8 5.6 %convolution_convert_fusion = bf16[4,200704]{1,0:T(4,128)(2,1)} fusion(bf16[2,200704]{1,0:T(2,128)(2,1)} %collective-permute-done.1, bf16[2,200704]{1,0:T(2,128)(2,1)} %bitcast.73, bf16[2,200704]{1,0:T(2,128)(2,1)} %collective-permute-done, s32[4]{0:T(128)S(1)} %fusion.36), kind=kOutput, calls=%fused_computation | convolution fusion | flops 17661976 | bytes 4014096 | tf_op jit(solution)/shard_map/dot_general | solution.py:84
  81.4 3.6 %reshape.139 = bf16[784,1024]{1,0:T(8,128)(2,1)} reshape(bf16[4,200704]{1,0:T(4,128)(2,1)} %convolution_convert_fusion) | data formatting | bytes 3211264 | tf_op jit(solution)/shard_map/reshape | solution.py:90
  85.0 4.3 %convert_reduce_fusion.1 = (f32[784]{0:T(1024)S(1)}, bf16[784,768]{1,0:T(8,128)(2,1)}) fusion(bf16[784,1024]{1,0:T(8,128)(2,1)} %reshape.139, bf16[128,8,768]{2,1,0:T(8,128)(2,1)} %all-to-all-done), kind=kOutput, calls=%fused_computation.21 | convolution fusion | flops 1234930944 | bytes 4385856 | tf_op jit(solution)/shard_map/dot_general | solution.py:91
  89.3 2.3 %reshape.141 = bf16[4,196,768]{2,1,0:T(8,128)(2,1)} reshape(bf16[784,768]{1,0:T(8,128)(2,1)} %get-tuple-element.15) | data formatting | bytes 2408448 | tf_op jit(solution)/shard_map/reshape | solution.py:94
  91.5 1.9 %fusion.16 = f32[784]{0:T(1024)S(1)} fusion(bf16[784,768]{1,0:T(8,128)(2,1)} %get-tuple-element.15, f32[784]{0:T(1024)S(1)} %broadcast_multiply_fusion.2), kind=kLoop, calls=%fused_computation.32 | loop fusion | flops 2407664 | bytes 1210496 | tf_op jit(solution)/shard_map/reduce_sum | solution.py:40
  93.5 1.4 fusion.17
  94.8 2.2 %dot_general.40 = bf16[4,196,768]{2,1,0:T(8,128)(2,1)} reshape(bf16[784,768]{1,0:T(8,128)(2,1)} %fusion.17) | data formatting | bytes 2408448 | tf_op jit(solution)/shard_map/dot_general | solution.py:47
  97.1 4.8 %convolution_convert_fusion.1 = bf16[4,196,2304]{2,1,0:T(8,128)(2,1)S(1)} fusion(bf16[4,196,768]{2,1,0:T(8,128)(2,1)} %dot_general.40, bf16[1,768,2304]{2,1,0:T(8,128)(2,1)S(1)} %copy-done), kind=kOutput, calls=%fused_computation.8 | convolution fusion | flops 2776338432 | bytes 8355840 | tf_op jit(solution)/shard_map/dot_general | solution.py:47
  101.9 1.9 %fusion.44 = (bf16[4,196,768]{2,1,0:T(8,128)(2,1)}, bf16[4,196,768]{2,1,0:T(8,128)(2,1)}, bf16[4,196,768]{2,1,0:T(8,128)(2,1)}) fusion(bf16[4,196,2304]{2,1,0:T(8,128)(2,1)S(1)} %convolution_convert_fusion.1), kind=kLoop, calls=%fused_computation.74 | loop fusion | bytes 7225344 | tf_op jit(solution)/shard_map/slice | solution.py:73
  103.8 1.6 copy.78
  105.4 2.5 %copy.79 = bf16[4,196,768]{1,2,0:T(8,128)(2,1)} copy(bf16[4,196,768]{2,1,0:T(8,128)(2,1)} %get-tuple-element.9) | data formatting | bytes 2408448 | tf_op jit(solution)/shard_map/slice | solution.py:73
  108.0 2.5 %copy.77 = bf16[4,196,768]{1,2,0:T(8,128)(2,1)} copy(bf16[4,196,768]{2,1,0:T(8,128)(2,1)} %get-tuple-element.11) | data formatting | bytes 2408448 | tf_op jit(solution)/shard_map/slice | solution.py:74
  110.5 2.9 %copy.82 = bf16[4,196,768]{2,0,1:T(4,128)(2,1)} copy(bf16[4,196,768]{2,1,0:T(8,128)(2,1)} %reshape.141) | data formatting | bytes 2408448 | tf_op jit(solution)/shard_map/reshape | solution.py:94
  113.4 1.5 collective-permute-start.2
  114.9 2.1 %fusion = (f32[4,12,196]{2,1,0:T(8,128)S(1)}, f32[4,12,196,196]{2,3,1,0:T(8,128)S(1)}) fusion(bf16[4,196,12,64]{1,3,2,0:T(8,128)(2,1)S(1)} %bitcast.65, bf16[4,196,12,64]{1,3,2,0:T(8,128)(2,1)S(1)} %bitcast.66), kind=kOutput, calls=%fused_computation.6 | convolution fusion | flops 239706432 | bytes 9821952 | tf_op jit(solution)/shard_map/bqhd,bkhd->bhqk/dot_general | solution.py:57
  117.1 2.4 %fusion.20 = bf16[4,12,64,196]{3,2,1,0:T(8,128)(2,1)S(1)} fusion(bf16[4,196,12,64]{1,3,2,0:T(8,128)(2,1)S(1)} %bitcast.68, f32[4,12,196,196]{2,3,1,0:T(8,128)S(1)} %get-tuple-element.17, f32[4,12,196]{2,1,0:T(8,128)S(1)} %get-tuple-element.16), kind=kOutput, calls=%fused_computation.36 | convolution fusion | flops 242161920 | bytes 9821952 | tf_op jit(solution)/shard_map/bhqk,bkhd->bqhd/dot_general | solution.py:62
  123.0 2.3 %convolution_convert_fusion.3 = bf16[4,196,768]{2,1,0:T(8,128)(2,1)} fusion(f32[4,196,768]{2,1,0:T(8,128)S(1)} %get-tuple-element.19, f32[4,196]{1,0:T(4,128)S(1)} %add_rsqrt_fusion.1, f32[4,196]{1,0:T(4,128)S(1)} %broadcast_multiply_fusion.1, bf16[1,768,768]{2,1,0:T(8,128)(2,1)S(1)} %copy-done.13), kind=kOutput, calls=%fused_computation.39 | convolution fusion | flops 927252480 | bytes 4798592 | tf_op jit(solution)/shard_map/dot_general | solution.py:47
  125.2 1.6 copy.89
  130.3 2.1 %convolution_convert_fusion.2 = bf16[4,196,1536]{2,1,0:T(8,128)(2,1)S(1)} fusion(bf16[1,768,1536]{2,1,0:T(8,128)(2,1)S(1)} %copy-done.11, bf16[4,196,768]{2,0,1:T(4,128)(2,1)S(1)} %fusion.15), kind=kOutput, calls=%fused_computation.12 | convolution fusion | flops 1850892288 | bytes 5971968 | tf_op jit(solution)/shard_map/dot_general | solution.py:47
  132.3 1.6 fusion.45
  134.0 2.5 %copy.90 = bf16[4,196,768]{1,2,0:T(8,128)(2,1)} copy(bf16[4,196,768]{2,1,0:T(8,128)(2,1)} %get-tuple-element.12) | data formatting | bytes 2408448 | tf_op jit(solution)/shard_map/slice | solution.py:79
  136.5 2.5 %copy.88 = bf16[4,196,768]{1,2,0:T(8,128)(2,1)} copy(bf16[4,196,768]{2,1,0:T(8,128)(2,1)} %get-tuple-element.13) | data formatting | bytes 2408448 | tf_op jit(solution)/shard_map/slice | solution.py:79
  139.0 3.6 %fusion.1 = (f32[4,12,196]{2,1,0:T(8,128)S(1)}, f32[4,12,196,196]{2,3,1,0:T(8,128)S(1)}) fusion(bf16[4,196,12,64]{1,3,2,0:T(8,128)(2,1)S(1)} %bitcast.64, bf16[4,196,12,64]{1,3,2,0:T(8,128)(2,1)} %bitcast.67), kind=kOutput, calls=%fused_computation.7 | convolution fusion | flops 239706432 | bytes 9821952 | tf_op jit(solution)/shard_map/bqhd,bkhd->bhqk/dot_general | solution.py:57
  142.7 2.4 %fusion.19 = bf16[4,12,64,196]{3,2,1,0:T(8,128)(2,1)S(1)} fusion(bf16[4,196,12,64]{1,3,2,0:T(8,128)(2,1)S(1)} %bitcast.69, f32[4,12,196,196]{2,3,1,0:T(8,128)S(1)} %get-tuple-element.21, f32[4,12,196]{2,1,0:T(8,128)S(1)} %get-tuple-element.20), kind=kOutput, calls=%fused_computation.35 | convolution fusion | flops 242161920 | bytes 9821952 | tf_op jit(solution)/shard_map/bhqk,bkhd->bqhd/dot_general | solution.py:62
  147.3 2.4 %convolution_bitcast_fusion = f32[1,6,150528]{2,1,0:T(8,128)S(1)} fusion(f32[4,150528]{1,0:T(4,128)S(1)} %bitcast.63, s32[4]{0:T(128)S(1)} %get-tuple-element.5), kind=kOutput, calls=%fused_computation.1 | convolution fusion | flops 43352088 | bytes 6021136 | tf_op jit(solution)/shard_map/dot_general | solution.py:141
  150.8 6.9 %collective-permute-start.4 = (f32[1,2,150528]{2,1,0:T(2,128)S(1)}, f32[1,2,150528]{2,1,0:T(2,128)S(1)}, u32[]{:S(2)}, u32[]{:S(2)}) collective-permute-start(f32[1,2,150528]{2,1,0:T(2,128)S(1)} %get-tuple-element.8), channel_id=1, source_target_pairs={{1,0},{2,1},{3,2},{4,3},{5,4},{6,5},{7,6},{8,7},{9,8},{10,9},{11,1... | collective-permute-start | bytes 3612680 | tf_op jit(solution)/shard_map/ppermute | solution.py:25
  157.7 26.6 %collective-permute-done.3 = f32[1,2,150528]{2,1,0:T(2,128)S(1)} collective-permute-done((f32[1,2,150528]{2,1,0:T(2,128)S(1)}, f32[1,2,150528]{2,1,0:T(2,128)S(1)}, u32[]{:S(2)}, u32[]{:S(2)}) %collective-permute-start.3) | collective-permute-done | bytes 1204256 | tf_op jit(solution)/shard_map/ppermute | solution.py:24
  184.3 2.0 %fusion.29 = f32[1,2,150528]{2,1,0:T(2,128)} fusion(f32[1,2,150528]{2,1,0:T(2,128)S(1)} %collective-permute-done.4, f32[1,2,150528]{2,1,0:T(2,128)S(1)} %collective-permute-done.3, f32[1,6,150528]{2,1,0:T(8,128)S(1)} %convolution_bitcast_fusion), kind=kLoop, calls=%fused_computation.45 | loop fusion | flops 602112 | bytes 4816896 | tf_op jit(solution)/shard_map/add | solution.py:153
  (50 shorter events, 10.7 us)
Async XLA Ops:
  0.0 97.1 %copy-start = (bf16[1,768,2304]{2,1,0:T(8,128)(2,1)S(1)}, bf16[1,768,2304]{2,1,0:T(8,128)(2,1)}, u32[]{:S(2)}) copy-start(bf16[1,768,2304]{2,1,0:T(8,128)(2,1)} %param.11) | copy-start | bytes 10616836
  2.1 24.0 %copy-start.10 = (s32[4,2]{0,1:T(2,128)S(1)}, s32[4,2]{0,1:T(2,128)}, u32[]{:S(2)}) copy-start(s32[4,2]{0,1:T(2,128)} %param.9) | copy-start | bytes 100
  2.1 82.8 %all-to-all-start = ((bf16[128,8,768]{2,1,0:T(8,128)(2,1)}), bf16[128,8,768]{2,1,0:T(8,128)(2,1)}, u32[]{:S(2)}, u32[]{:S(2)}) async-start(bf16[128,8,768]{2,1,0:T(8,128)(2,1)} %stack.4), calls=%async_computation | async-start | bytes 3145728 | tf_op jit(solution)/shard_map/all_to_all | solution.py:13
  19.1 56.7 %collective-permute-start = (bf16[2,200704]{1,0:T(2,128)(2,1)}, bf16[2,200704]{1,0:T(2,128)(2,1)}, u32[]{:S(2)}, u32[]{:S(2)}) collective-permute-start(bf16[2,200704]{1,0:T(2,128)(2,1)} %bitcast.71), channel_id=1, source_target_pairs={{0,1},{1,2},{2,3},{3,4},{4,5},{5,6},{6,7},{7,8},{8,9},{9,10},{10,1... | collective-permute-start | bytes 2408456 | tf_op jit(solution)/shard_map/ppermute | solution.py:24
  19.6 56.1 %collective-permute-start.1 = (bf16[2,200704]{1,0:T(2,128)(2,1)}, bf16[2,200704]{1,0:T(2,128)(2,1)}, u32[]{:S(2)}, u32[]{:S(2)}) collective-permute-start(bf16[2,200704]{1,0:T(2,128)(2,1)} %bitcast.72), channel_id=1, source_target_pairs={{1,0},{2,1},{3,2},{4,3},{5,4},{6,5},{7,6},{8,7},{9,8},{10,9},{11,1... | collective-permute-start | bytes 2408456 | tf_op jit(solution)/shard_map/ppermute | solution.py:25
  91.5 1.9 %copy-start.2 = (bf16[784,768]{1,0:T(8,128)(2,1)S(1)}, bf16[784,768]{1,0:T(8,128)(2,1)}, u32[]{:S(2)}) copy-start(bf16[784,768]{1,0:T(8,128)(2,1)} %get-tuple-element.15) | copy-start | bytes 3612676
  110.5 4.4 %copy-start.5 = (bf16[4,196,768]{1,2,0:T(8,128)(2,1)S(1)}, bf16[4,196,768]{1,2,0:T(8,128)(2,1)}, u32[]{:S(2)}) copy-start(bf16[4,196,768]{1,2,0:T(8,128)(2,1)} %copy.79) | copy-start | bytes 3612676
  113.4 13.5 %collective-permute-start.2 = (bf16[4,196,768]{2,0,1:T(4,128)(2,1)}, bf16[4,196,768]{2,0,1:T(4,128)(2,1)S(1)}, u32[]{:S(2)}, u32[]{:S(2)}) collective-permute-start(bf16[4,196,768]{2,0,1:T(4,128)(2,1)} %copy.82), channel_id=1, source_target_pairs={{0,128},{128,0},{1,129},{129,1},{2,130},{130,2},{3,131},{131,3},{4... | collective-permute-start | bytes 3612680 | tf_op jit(solution)/shard_map/ppermute | solution.py:33
  114.9 2.1 %copy-start.7 = (bf16[4,196,768]{1,2,0:T(8,128)(2,1)S(1)}, bf16[4,196,768]{1,2,0:T(8,128)(2,1)}, u32[]{:S(2)}) copy-start(bf16[4,196,768]{1,2,0:T(8,128)(2,1)} %copy.77) | copy-start | bytes 3612676
  117.1 2.4 %copy-start.6 = (bf16[4,196,768]{2,1,0:T(8,128)(2,1)S(1)}, bf16[4,196,768]{2,1,0:T(8,128)(2,1)}, u32[]{:S(2)}) copy-start(bf16[4,196,768]{2,1,0:T(8,128)(2,1)} %reshape.141) | copy-start | bytes 3612676
  117.1 2.4 %copy-start.12 = (bf16[1,768,768]{2,1,0:T(8,128)(2,1)S(1)}, bf16[1,768,768]{2,1,0:T(8,128)(2,1)}, u32[]{:S(2)}) copy-start(bf16[1,768,768]{2,1,0:T(8,128)(2,1)} %param.12) | copy-start | bytes 3538948
  120.8 1.4 copy-start.3
  120.8 2.1 %copy-start.13 = (bf16[1,768,768]{2,1,0:T(8,128)(2,1)S(1)}, bf16[1,768,768]{2,1,0:T(8,128)(2,1)}, u32[]{:S(2)}) copy-start(bf16[1,768,768]{2,1,0:T(8,128)(2,1)} %param.13) | copy-start | bytes 3538948
  128.6 1.7 copy-start.11
  139.0 3.7 %copy-start.8 = (bf16[4,196,768]{1,2,0:T(8,128)(2,1)S(1)}, bf16[4,196,768]{1,2,0:T(8,128)(2,1)}, u32[]{:S(2)}) copy-start(bf16[4,196,768]{1,2,0:T(8,128)(2,1)} %copy.88) | copy-start | bytes 3612676
  142.7 2.4 %copy-start.4 = (f32[4,196,768]{2,1,0:T(8,128)S(1)}, f32[4,196,768]{2,1,0:T(8,128)}, u32[]{:S(2)}) copy-start(f32[4,196,768]{2,1,0:T(8,128)} %copy-done.3) | copy-start | bytes 7225348
  142.7 2.4 %copy-start.9 = (bf16[1,768,768]{2,1,0:T(8,128)(2,1)S(1)}, bf16[1,768,768]{2,1,0:T(8,128)(2,1)}, u32[]{:S(2)}) copy-start(bf16[1,768,768]{2,1,0:T(8,128)(2,1)} %param.15) | copy-start | bytes 3538948
  150.7 33.6 %collective-permute-start.3 = (f32[1,2,150528]{2,1,0:T(2,128)S(1)}, f32[1,2,150528]{2,1,0:T(2,128)S(1)}, u32[]{:S(2)}, u32[]{:S(2)}) collective-permute-start(f32[1,2,150528]{2,1,0:T(2,128)S(1)} %get-tuple-element.7), channel_id=1, source_target_pairs={{0,1},{1,2},{2,3},{3,4},{4,5},{5,6},{6,7},{7,8},{8,9},{9,10},{10,1... | collective-permute-start | bytes 3612680 | tf_op jit(solution)/shard_map/ppermute | solution.py:24
  150.8 35.5 %copy-start.1 = (bf16[1,768,2304]{2,1,0:T(8,128)(2,1)S(1)}, bf16[1,768,2304]{2,1,0:T(8,128)(2,1)}, u32[]{:S(2)}) copy-start(bf16[1,768,2304]{2,1,0:T(8,128)(2,1)} %param.11) | copy-start | bytes 10616836
  150.8 33.5 %collective-permute-start.4 = (f32[1,2,150528]{2,1,0:T(2,128)S(1)}, f32[1,2,150528]{2,1,0:T(2,128)S(1)}, u32[]{:S(2)}, u32[]{:S(2)}) collective-permute-start(f32[1,2,150528]{2,1,0:T(2,128)S(1)} %get-tuple-element.8), channel_id=1, source_target_pairs={{1,0},{2,1},{3,2},{4,3},{5,4},{6,5},{7,6},{8,7},{9,8},{10,9},{11,1... | collective-permute-start | bytes 3612680 | tf_op jit(solution)/shard_map/ppermute | solution.py:25
